TPU v7x, 32 devices: a whole 2x2x4 slice. The times are simulated.
32 devices in a mesh: row: 4 (over y, core), col: 8 (over z, x).
Axes of the slice: x: 2, y: 2, z: 4, core: 2. Of those that a mesh axis runs over, the one named last changes fastest.
Arguments:
- near_blocks: bfloat16 [64, 16, 512, 512], P(('row', 'col')), may hold values from -2 to 9, as said below
- leaf_basis: bfloat16 [64, 512, 512], P(('row', 'col')), may hold values from -1 to 2, as said below
- near_cols: int32 [64, 16], P(('row', 'col')), may hold values from 0 to 63, as said below
- near_count: int32 [64], P(('row', 'col')), may hold values from 1 to 16, as said below
- children: int32 [32, 2], replicated, may hold values from 0 to 63, as said below
- parent_basis: bfloat16 [32, 256, 256], P(('row', 'col')), may hold values from -1 to 2, as said below
- far_coupling: float32 [32, 128, 128], P(('row', 'col')), may hold values from -0.25 to 0.25
Outputs:
- leaf_factor: float32 [64, 384, 384], P(('row', 'col'))
- near_schur: float32 [64, 16, 128, 128], P(('row', 'col'))
- top_factor: float32 [32, 128, 128], P(('row', 'col'))
- top_schur: float32 [32, 128, 128], P(('row', 'col'))
Inputs may be any that keep to these rules, and one draw needn't show every extreme that they name: near_cols[i, 0] = i; for 1 <= t < near_count[i] the entries near_cols[i, t] are distinct leaves other than i of i's group, the leaves 16 * g to 16 * g + 15 with g = i // 16; slots t >= near_count[i] hold i. `near_count`: some leaf has 16 live slots. Parent p belongs to group g = 2 * p // 16; children[p, 0] is a leaf of group g and children[p, 1] a leaf of group g + 1 - 2 * (g % 2); every leaf is a child of exactly one parent. near_blocks[i, 0] is symmetric positive definite. `leaf_basis`: each basis is nonsingular. `parent_basis`: each basis is nonsingular.
All inputs are finite; a program needn't handle non-finite values.
Results may differ from a plain program's by a relative error of at most 0.0015.
Values may be sent and summed in bfloat16 or wider, within the bound.
A program may use at most 192 MiB of HBM per device.

v0:
```python
from functools import partial

import jax
import jax.numpy as jnp
from jax import lax
from jax.sharding import PartitionSpec as P

HIGHEST = lax.Precision.HIGHEST


def for_sending(x):

    def short(part):
        return part.astype(jnp.bfloat16) if part.dtype == jnp.float32 else part

    return jax.tree.map(short, x)


def swapped(block, axis, distance):
    count = lax.axis_size(axis)
    route = []
    for low in range(count):
        high = low | 1 << distance
        if high != low and high < count:
            route += [(low, high), (high, low)]
    return lax.ppermute(block, axis, route)


def rotate_pivot(near_block, basis, red_size):
    product = jnp.dot(near_block, basis, preferred_element_type=jnp.float32)
    rotated = jnp.dot(basis.astype(jnp.float32).T, product, precision=HIGHEST)
    factor = jnp.linalg.cholesky(rotated[:red_size, :red_size])
    pivot = jax.scipy.linalg.cho_solve((factor, True), rotated[:red_size, red_size:])
    self_schur = rotated[red_size:, red_size:] - jnp.dot(
        rotated[red_size:, :red_size], pivot, precision=HIGHEST
    )
    return (factor, pivot, self_schur)


def pair_folded(near_block, own_float, own_pivot, other_panel, other_rest, red_size):
    skel_rank = other_rest.shape[1]
    product = jnp.dot(near_block, other_panel, preferred_element_type=jnp.float32)
    rest_part = jnp.dot(near_block, other_rest, preferred_element_type=jnp.float32)
    corrected_part = product[:, :skel_rank] + rest_part
    first_term = jnp.dot(own_float[:, red_size:].T, corrected_part, precision=HIGHEST)
    red_rows = jnp.dot(own_float[:, :red_size].T, product[:, skel_rank:], precision=HIGHEST)
    return first_term - jnp.dot(own_pivot.T, red_rows, precision=HIGHEST)


def local(near_blocks, leaf_basis, near_cols, near_count, children, parent_basis, far_coupling):
    local_leaves, slots = near_cols.shape
    leaf_size = leaf_basis.shape[1]
    skel_rank = far_coupling.shape[1]
    red_size = leaf_size - skel_rank
    factors, pivots, diag_schur = jax.vmap(partial(rotate_pivot, red_size=red_size))(
        near_blocks[:, 0], leaf_basis
    )
    row_index = lax.axis_index("row")
    col_index = lax.axis_index("col")
    col_count = lax.axis_size("col")
    group_size = local_leaves * col_count
    group_base = row_index * group_size
    basis_float = leaf_basis.astype(jnp.float32)
    corrected = basis_float[:, :, red_size:] - jnp.einsum(
        "lrk,lkc->lrc", basis_float[:, :, :red_size], pivots, precision=HIGHEST
    )
    gathered_corr = lax.all_gather(for_sending(corrected), "col", axis=0, tiled=True).astype(
        corrected.dtype
    )
    gathered_skel = lax.all_gather(leaf_basis[:, :, red_size:], "col", axis=0, tiled=True)
    upper_part = gathered_corr.astype(jnp.bfloat16)
    other_second = (gathered_corr - upper_part.astype(jnp.float32)).astype(jnp.bfloat16)
    other_first = jnp.concatenate([upper_part, gathered_skel], axis=2)
    slot_ids = jnp.arange(slots, dtype=jnp.int32)
    schur_list = []
    for local_leaf in range(local_leaves):
        own_float = leaf_basis[local_leaf].astype(jnp.float32)
        own_pivot = pivots[local_leaf]

        def slot_term(slot_args, own_float=own_float, own_pivot=own_pivot):
            near_block, near_column = slot_args
            offset = near_column - group_base
            return pair_folded(
                near_block,
                own_float,
                own_pivot,
                other_first[offset],
                other_second[offset],
                red_size,
            )

        terms = lax.map(slot_term, (near_blocks[local_leaf, 1:], near_cols[local_leaf, 1:]))
        schur_rows = jnp.concatenate([diag_schur[local_leaf][None], terms], axis=0)
        live = slot_ids < near_count[local_leaf]
        schur_rows = jnp.where(live[:, None, None], schur_rows, jnp.float32(0.0))
        schur_list.append(schur_rows)
    near_schur = jnp.stack(schur_list, axis=0)
    child_all = lax.all_gather(diag_schur, "col", axis=0, tiled=True)
    partner_row = row_index + 1 - 2 * (row_index % 2)
    parent_id = row_index * col_count + col_index
    first_block = child_all[children[parent_id, 0] - group_base]
    partner_parent = partner_row * col_count + col_index
    outgoing = child_all[children[partner_parent, 1] - group_base]
    second_block = swapped(outgoing, "row", 0)
    coupling = far_coupling[0]
    upper = jnp.concatenate([first_block, coupling], axis=1)
    lower = jnp.concatenate([coupling.T, second_block], axis=1)
    merged = jnp.concatenate([upper, lower], axis=0)
    parent_float = parent_basis[0].astype(jnp.float32)
    rotated = jnp.dot(
        parent_float.T, jnp.dot(merged, parent_float, precision=HIGHEST), precision=HIGHEST
    )
    top_chol = jnp.linalg.cholesky(rotated[:skel_rank, :skel_rank])
    solved = jax.scipy.linalg.cho_solve((top_chol, True), rotated[:skel_rank, skel_rank:])
    top_block = rotated[skel_rank:, skel_rank:] - jnp.dot(
        rotated[skel_rank:, :skel_rank], solved, precision=HIGHEST
    )
    return (factors, near_schur, top_chol[None], top_block[None])


def solution(mesh):
    placed = (
        P(("row", "col"), None, None, None),
        P(("row", "col"), None, None),
        P(("row", "col"), None),
        P(("row", "col")),
        P(),
        P(("row", "col"), None, None),
        P(("row", "col"), None, None),
    )
    return jax.shard_map(
        local,
        mesh=mesh,
        in_specs=placed,
        out_specs=(
            P(("row", "col"), None, None),
            P(("row", "col"), None, None, None),
            P(("row", "col"), None, None),
            P(("row", "col"), None, None),
        ),
        check_vma=False,
    )
```

profile of v0, /device:TPU:0, one launch (start us, length us, event | category | flops | bytes accessed | tf_op | source)
XLA Modules:
  0.0 585.7 jit_solution(10955401701314171731)
XLA Ops:
  9.1 2.4 fusion.38
  11.5 1.8 convolution_bitcast_fusion
  14.4 2.7 copy.98
  17.0 1.4 fusion.36
  20.2 24.4 %custom-call.39 = f32[2,128,128]{2,1,0:T(8,128)S(1)} custom-call(f32[2,128,128]{2,1,0:T(8,128)} %cholesky.248), custom_call_target="Cholesky" | custom-call | tf_op jit(solution)/shard_map/vmap(jit(cholesky))/cholesky | solution.py:32
  46.0 21.1 %custom-call.40 = f32[2,1,128,128]{2,3,1,0:T(8,128)} custom-call(f32[2,1,128,128]{3,2,1,0:T(8,128)} %select_bitcast_fusion.1), custom_call_target="InvertDiagBlocksLowerTriangular" | custom-call | tf_op jit(solution)/shard_map/vmap(jit(cholesky))/cholesky | solution.py:32
  68.2 2.1 constant_dynamic-update-slice_fusion.6
  72.9 24.9 %custom-call.41 = f32[2,128,128]{2,1,0:T(8,128)} custom-call(f32[2,128,128]{2,1,0:T(8,128)} %cholesky.252), custom_call_target="Cholesky" | custom-call | tf_op jit(solution)/shard_map/vmap(jit(cholesky))/cholesky | solution.py:32
  97.8 1.6 select_bitcast_fusion
  99.4 21.5 %custom-call.42 = f32[2,1,128,128]{2,3,1,0:T(8,128)} custom-call(f32[2,1,128,128]{3,2,1,0:T(8,128)} %get-tuple-element.204), custom_call_target="InvertDiagBlocksLowerTriangular" | custom-call | tf_op jit(solution)/shard_map/vmap(jit(cholesky))/cholesky | solution.py:32
  120.9 1.9 convolution_dynamic-update-slice_fusion
  122.8 2.1 convolution_subtract_fusion.6
  124.9 24.9 %custom-call.43 = f32[2,128,128]{2,1,0:T(8,128)} custom-call(f32[2,128,128]{2,1,0:T(8,128)} %convolution_subtract_fusion.6), custom_call_target="Cholesky" | custom-call | tf_op jit(solution)/shard_map/vmap(jit(cholesky))/cholesky | solution.py:32
  149.8 2.2 select_reduce_fusion.1
  153.0 2.9 broadcast_select_fusion
  155.9 10.8 %while.23 = (s32[]{:T(128)}, f32[2,384,384]{2,1,0:T(8,128)}, s32[3,2]{0,1:T(2,128)S(1)}, f32[3,2,128,128]{3,2,0,1:T(8,128)}, s32[]{:T(128)}) while((s32[]{:T(128)}, f32[2,384,384]{2,1,0:T(8,128)}, s32[3,2]{0,1:T(2,128)S(1)}, f32[3,2,128,128]{3,2,0,1:T(8,128)}, s32[]{:T(128)}) %tuple.71), condition=%wide.while_cond, body=%wide.while_body.sunk | while | flops 2 | bytes 263777 | solution.py:33
  156.6 3.0 bitcast_dynamic-update-slice_fusion.2
  160.2 3.0 bitcast_dynamic-update-slice_fusion.2
  163.8 2.9 bitcast_dynamic-update-slice_fusion.2
  166.8 60.4 %custom-call.44 = f32[2,3,128,128]{2,3,1,0:T(8,128)} custom-call(f32[2,3,128,128]{3,2,1,0:T(8,128)} %bitcast.208), custom_call_target="InvertDiagBlocksLowerTriangular" | custom-call | tf_op jit(solution)/shard_map/vmap(jit(_cho_solve))/triangular_solve | solution.py:33
  231.1 1.6 convolution_subtract_fusion.5
  235.0 1.6 convolution_subtract_fusion.4
  237.6 1.5 convolution_subtract_fusion.3
  239.0 1.6 copy.124
  241.0 1.9 fusion.35
  251.0 11.3 %slice_bitcast_fusion.1 = (bf16[15,512,512]{2,1,0:T(8,128)(2,1)}, bf16[15,512,512]{2,1,0:T(8,128)(2,1)}) fusion(bf16[2,16,512,512]{3,2,1,0:T(8,128)(2,1)} %param.11), kind=kLoop, calls=%fused_computation.43 | loop fusion | bytes 31457280 | tf_op jit(solution)/shard_map/squeeze | solution.py:92
  262.3 21.5 %all-gather.8.cloned.1.call-done = f32[16,128,128]{2,1,0:T(8,128)} async-done(((f32[2,128,128]{2,1,0:T(8,128)}), f32[16,128,128]{2,1,0:T(8,128)}) %all-gather.8.cloned.1.call-update) | async-done | bytes 1048592 | tf_op jit(solution)/shard_map/all_gather | solution.py:98
  286.8 11.7 %cholesky.239 = f32[128,128]{1,0:T(8,128)S(1)} custom-call(f32[128,128]{1,0:T(8,128)S(1)} %fusion.83), custom_call_target="Cholesky" | custom-call | tf_op jit(solution)/shard_map/jit(cholesky)/cholesky | solution.py:113
  300.5 9.8 %custom-call.45 = f32[1,128,128]{1,2,0:T(8,128)S(1)} custom-call(f32[1,128,128]{2,1,0:T(8,128)S(1)} %get-tuple-element.206), custom_call_target="InvertDiagBlocksLowerTriangular" | custom-call | tf_op jit(solution)/shard_map/jit(_cho_solve)/triangular_solve | solution.py:114
  311.9 22.3 %all-gather.4.cloned.1.call-done = bf16[16,512,128]{2,1,0:T(8,128)(2,1)} async-done(((bf16[2,512,128]{2,1,0:T(8,128)(2,1)}), bf16[16,512,128]{2,1,0:T(8,128)(2,1)}) %all-gather.4.cloned.1.call-update) | async-done | bytes 2097168 | tf_op jit(solution)/shard_map/all_gather | solution.py:67
  334.2 3.3 constant_dynamic-update-slice_fusion.3
  337.5 1.9 subtract_convert_fusion
  339.3 44.6 %all-gather.6.cloned.1.call-done = bf16[16,512,128]{2,1,0:T(8,128)(2,1)} async-done(((bf16[2,512,128]{2,1,0:T(8,128)(2,1)}), bf16[16,512,128]{2,1,0:T(8,128)(2,1)}) %all-gather.6.cloned.1.call-update) | async-done | bytes 2097168 | tf_op jit(solution)/shard_map/all_gather | solution.py:70
  383.9 3.2 constant_dynamic-update-slice_fusion.2
  388.2 98.2 %while.21 = (s32[]{:T(128)}, f32[15,128,128]{2,1,0:T(8,128)}, bf16[15,512,512]{2,1,0:T(8,128)(2,1)}, s32[15]{0:T(128)S(1)}, s32[]{:T(128)}, /*index=5*/bf16[16,5...) while((s32[]{:T(128)}, f32[15,128,128]{2,1,0:T(8,128)}, ...), condition=%wide.region_7.8_spmd, body=%wide.region_6.7_spmd.sunk | while | flops 679559168 | bytes 5113527 | solution.py:92
  396.1 1.4 fusion.149
  441.9 1.4 fusion.149
  455.0 1.4 fusion.149
  468.1 1.4 fusion.149
  481.1 1.4 fusion.149
  486.4 89.5 %while.22 = (s32[]{:T(128)}, f32[15,128,128]{2,1,0:T(8,128)S(1)}, bf16[15,512,512]{2,1,0:T(8,128)(2,1)}, s32[15]{0:T(128)S(1)}, s32[]{:T(128)}, /*index=5*/bf16[...) while((s32[]{:T(128)}, f32[15,128,128]{2,1,0:T(8,128)S(1)}, ...), condition=%wide.region_9.10_spmd, body=%wide.region_8.9_spmd.sunk | while | flops 679559168 | bytes 5113019 | solution.py:92
  488.0 1.4 fusion.163
  494.0 1.4 fusion.163
  499.9 1.4 fusion.163
  523.7 1.4 fusion.163
  529.7 1.4 fusion.163
  553.5 1.4 fusion.163
  577.5 1.5 pad_maximum_fusion
  (328 shorter events, 185.4 us)
Async XLA Ops:
  7.2 278.9 %copy-start = (bf16[1,256,256]{2,1,0:T(8,128)(2,1)S(1)}, bf16[1,256,256]{2,1,0:T(8,128)(2,1)}, u32[]{:S(2)}) copy-start(bf16[1,256,256]{2,1,0:T(8,128)(2,1)} %param.16) | copy-start | bytes 393220
  7.2 276.7 %all-gather.8.cloned.1.call-start = ((), (), s32[]{:S(2)}) async-start(), calls=%async_computation.2 | async-start | bytes 1179648 | tf_op jit(solution)/shard_map/all_gather | solution.py:98
  9.1 2.4 copy-start.2
  18.5 1.0 copy-start.4
  71.6 0.7 copy-start.9
  152.1 3.9 copy-start.14
  227.2 5.6 copy-start.6
  236.9 0.7 copy-start.7
  240.7 3.8 copy-start.12
  240.7 5.7 copy-start.8
  240.7 93.5 %all-gather.4.cloned.1.call-start = ((), (), s32[]{:S(2)}) async-start(), calls=%async_computation | async-start | bytes 2359296 | tf_op jit(solution)/shard_map/all_gather | solution.py:67
  240.8 2.9 copy-start.5
  243.7 140.2 %all-gather.6.cloned.1.call-start = ((), (), s32[]{:S(2)}) async-start(), calls=%async_computation.1 | async-start | bytes 2359296 | tf_op jit(solution)/shard_map/all_gather | solution.py:70
  247.1 1.2 copy-start.10
  247.1 2.3 copy-start.13
  247.1 2.5 copy-start.11
  284.7 1.3 collective-permute-start
  334.2 3.3 copy-start.3
  577.3 1.6 copy-start.1
Sparse Core Ops, SparseCore 0:
  240.8 42.9 all-gather.7
  286.0 48.1 all-gather.3
  336.3 47.5 all-gather.5
where the time goes:
time: 591 us; the launch traced here: 586 us
  other arithmetic  220 us (37%)
  matrix products  159 us (27%)
  waiting for transfers between devices  89.7 us (15%)
  local copies, waits for them, and re-layouts  78.3 us (13%)
  loops' own time  22.6 us (4%)
  between operations  15.7 us (3%)
    another operation x13, other arithmetic, rotate_pivot(): factor = jnp.linalg.cholesky(rotated[:red_size, :red_size])  124 us
    another operation x4, other arithmetic, rotate_pivot(): jax.scipy.linalg.cho_solve((factor, True), rotated[:red_size, red_size:])  64.6 us
    all_gather x1, waiting for transfers between devices, local(): lax.all_gather(leaf_basis[:, :, red_size:], 'col', axis=0, tiled=True)  44.6 us
    dot_general x30, matrix products, pair_folded(): jnp.dot(near_block, other_panel, preferred_element_type=jnp.float32)  42.3 us
    dot_general x30, matrix products, pair_folded(): jnp.dot(near_block, other_rest, preferred_element_type=jnp.float32)  40.7 us
    another operation x2, loops' own time, local(): lax.map(slot_term, (near_blocks[local_leaf, 1:], near_cols[local_leaf, 1:]))  22.6 us
    dot_general x30, matrix products, pair_folded(): jnp.dot(own_float[:, :red_size].T, product[:, skel_rank:], precision=HIGH...  22.4 us
    all_gather x1, waiting for transfers between devices, local(): lax.all_gather(for_sending(corrected), 'col', axis=0, tiled=True)  22.3 us
  transfers between devices with their start and end apart: 4, of which 4 were waited for; matrix products, arithmetic and copies ran while one was open for 9% of the time, Pallas kernels for 0%

commit v1 on v0

v1 whole, which is shorter than its diff:
```python
from functools import partial

import jax
import jax.numpy as jnp
from jax import lax
from jax.experimental import pallas as pl
from jax.experimental.pallas import tpu as pltpu
from jax.sharding import PartitionSpec as P

F32 = jnp.float32
BF16 = jnp.bfloat16
SUB = 8
NN = (((1,), (0,)), ((), ()))
NT = (((1,), (1,)), ((), ()))


def split(x):
    high = x.astype(BF16)
    return high, (x - high.astype(F32)).astype(BF16)


def mul(a, b, dims):
    return lax.dot_general(a, b, dims, preferred_element_type=F32)


def mul_three(a, b, dims):
    a_high, a_low = split(a)
    b_high, b_low = split(b)
    return mul(a_high, b_high, dims) + (mul(a_high, b_low, dims) + mul(a_low, b_high, dims))


def over_rows(x, k, width):
    return jnp.broadcast_to(x[k : k + 1, :], (SUB, width))


def factor_blocks(mats):
    order = mats[0].shape[0]
    count = order // SUB
    lane = lax.broadcasted_iota(jnp.int32, (SUB, order), 1)
    sub = lax.broadcasted_iota(jnp.int32, (SUB, order), 0)
    works = [[m[b * SUB : (b + 1) * SUB, :] for b in range(count)] for m in mats]
    uppers = [[] for _ in mats]
    inverses = [[] for _ in mats]
    for s in range(count):
        first = s * SUB
        inside = (lane >= first) & (lane < first + SUB)
        unit = jnp.where(lane == sub + first, F32(1.0), F32(0.0))
        columns = []
        pivots = []
        for work in works:
            columns.append(
                [
                    {
                        b: jnp.broadcast_to(work[b][:, first + n : first + n + 1], (SUB, order))
                        for b in range(s, count)
                    }
                    for n in range(SUB)
                ]
            )
            pivots.append(jnp.ones((SUB, order), F32))
            for b in range(s, count):
                work[b] = jnp.where(inside, unit if b == s else F32(0.0), work[b])
        for k in range(SUB):
            for which, work in enumerate(works):
                column = columns[which]
                pivot = over_rows(column[k][s], k, order)
                inverse = pl.reciprocal(pivot, approx=False)
                pivots[which] = jnp.where(sub == k, pivot, pivots[which])
                step = {b: column[k][b] * inverse for b in range(s, count)}
                step[s] = jnp.where(sub > k, step[s], F32(0.0))
                for n in range(k + 1, SUB):
                    value = over_rows(column[n][s], k, order)
                    for b in range(s, count):
                        column[n][b] = column[n][b] - step[b] * value
                row = over_rows(work[s], k, order)
                for b in range(s, count):
                    work[b] = work[b] - step[b] * row
        for which, work in enumerate(works):
            value = pivots[which]
            scale = lax.rsqrt(value)
            scale = scale * (F32(1.5) - F32(0.5) * value * scale * scale)
            upper = work[s]
            for n in range(SUB):
                upper = jnp.where(lane == first + n, columns[which][n][s], upper)
            upper = jnp.where(lane >= sub + first, upper, F32(0.0))
            uppers[which].append(upper * scale)
            inverses[which].append(
                jnp.where(lane <= sub + first, work[s], F32(0.0)) * scale
            )
    lowers = [jnp.concatenate(rows, axis=0).T for rows in uppers]
    inverse_lowers = [jnp.concatenate(rows, axis=0) for rows in inverses]
    return lowers, inverse_lowers


def leaf_kernel(near_ref, basis_ref, factor_ref, schur_ref, rows_ref, work, inv, turned):
    leaves = basis_ref.shape[0]
    block = schur_ref.shape[1]
    parts = basis_ref.shape[1] // block
    red = parts - 1
    for leaf in range(leaves):
        basis = basis_ref[leaf]
        turned[leaf] = basis.T
        high, low = split(mul(near_ref[leaf, 0], basis, NN))
        for i in range(parts):
            left = turned[leaf, i * block : (i + 1) * block, :]
            for j in range(i + 1):
                cut = slice(j * block, (j + 1) * block)
                work[leaf, i, j] = mul(left, high[:, cut], NN) + mul(left, low[:, cut], NN)
        for i in range(red):
            for j in range(i + 1, red):
                factor_ref[
                    leaf, i * block : (i + 1) * block, j * block : (j + 1) * block
                ] = jnp.zeros((block, block), F32)

    def eliminate(k, _):
        lowers, inverses = factor_blocks([work[leaf, k, k] for leaf in range(leaves)])
        for leaf in range(leaves):
            work[leaf, k, k] = lowers[leaf]
            inv[leaf, k] = inverses[leaf]
        for i in range(1, parts):

            @pl.when(i > k)
            def _(i=i):
                for leaf in range(leaves):
                    work[leaf, i, k] = mul_three(work[leaf, i, k], inv[leaf, k], NT)

        for i in range(1, parts):
            for j in range(1, i + 1):

                @pl.when(j > k)
                def _(i=i, j=j):
                    for leaf in range(leaves):
                        work[leaf, i, j] = work[leaf, i, j] - mul_three(
                            work[leaf, i, k], work[leaf, j, k], NT
                        )

        return 0

    lax.fori_loop(0, red, eliminate, 0)
    for leaf in range(leaves):
        for i in range(red):
            for j in range(i + 1):
                factor_ref[
                    leaf, i * block : (i + 1) * block, j * block : (j + 1) * block
                ] = work[leaf, i, j]
        schur_ref[leaf] = work[leaf, red, red]
        solved = {}
        total = jnp.zeros((block, basis_ref.shape[1]), F32)
        for k in reversed(range(red)):
            value = work[leaf, red, k]
            for m in range(k + 1, red):
                value = value - mul_three(solved[m], work[leaf, m, k], NN)
            solved[k] = mul_three(value, inv[leaf, k], NN)
            high, low = split(solved[k])
            right = turned[leaf, k * block : (k + 1) * block, :]
            total = total + (mul(high, right, NN) + mul(low, right, NN))
        rows_ref[leaf, :block, :] = turned[leaf, red * block :, :]
        rows_ref[leaf, block:, :] = total.astype(BF16)


def leaf_stage(near_blocks, leaf_basis, block):
    leaves, size = leaf_basis.shape[:2]
    red_size = size - block
    parts = size // block
    return pl.pallas_call(
        leaf_kernel,
        grid=(1,),
        in_specs=[
            pl.BlockSpec((leaves, 1, size, size), lambda g: (0, 0, 0, 0)),
            pl.BlockSpec((leaves, size, size), lambda g: (0, 0, 0)),
        ],
        out_specs=[
            pl.BlockSpec((leaves, red_size, red_size), lambda g: (0, 0, 0)),
            pl.BlockSpec((leaves, block, block), lambda g: (0, 0, 0)),
            pl.BlockSpec((leaves, 2 * block, size), lambda g: (0, 0, 0)),
        ],
        out_shape=[
            jax.ShapeDtypeStruct((leaves, red_size, red_size), F32),
            jax.ShapeDtypeStruct((leaves, block, block), F32),
            jax.ShapeDtypeStruct((leaves, 2 * block, size), BF16),
        ],
        scratch_shapes=[
            pltpu.VMEM((leaves, parts, parts, block, block), F32),
            pltpu.VMEM((leaves, parts - 1, block, block), F32),
            pltpu.VMEM((leaves, size, size), BF16),
        ],
        compiler_params=pltpu.CompilerParams(vmem_limit_bytes=40 << 20),
        cost_estimate=pl.CostEstimate(
            flops=40_000_000_000, bytes_accessed=6_000_000, transcendentals=0
        ),
        name="leaf_stage",
    )(near_blocks, leaf_basis)


DEPTH = 4


def near_kernel(
    cols_ref, count_ref, base_ref, near_ref, own_ref, skel_ref, turned_ref, diag_ref, out_ref, buf, sems
):
    leaves = own_ref.shape[0]
    block = diag_ref.shape[1]
    first = count_ref[0] - 1
    total = first
    for leaf in range(1, leaves):
        total = total + count_ref[leaf] - 1

    def place(w):
        leaf = jnp.int32(0)
        slot = w
        for other in range(leaves - 1):
            span = count_ref[other] - 1
            past = (leaf == other) & (slot >= span)
            slot = jnp.where(past, slot - span, slot)
            leaf = jnp.where(past, leaf + 1, leaf)
        return leaf, slot + 1

    def copy_of(w):
        leaf, slot = place(w)
        at = lax.rem(w, DEPTH)
        return pltpu.make_async_copy(near_ref.at[leaf, slot], buf.at[at], sems.at[at])

    for w in range(DEPTH - 1):

        @pl.when(w < total)
        def _(w=w):
            copy_of(jnp.int32(w)).start()

    out_ref[...] = jnp.zeros_like(out_ref)
    for leaf in range(leaves):
        out_ref[leaf, 0] = diag_ref[leaf]

    def body(w, _):
        @pl.when(w + DEPTH - 1 < total)
        def _():
            copy_of(w + DEPTH - 1).start()

        copy_of(w).wait()
        leaf, slot = place(w)
        other = cols_ref[leaf, slot] - base_ref[0]
        left = mul(own_ref[leaf], buf[lax.rem(w, DEPTH)], NN)
        skel_rows = left[:block]
        mixed = (skel_rows - left[block:]).astype(BF16)
        out_ref[leaf, slot] = mul(mixed, skel_ref[other], NN) - mul(
            skel_rows.astype(BF16), turned_ref[other], NT
        )
        return 0

    lax.fori_loop(0, total, body, 0)


def near_stage(near_blocks, near_cols, near_count, base, own_rows, skel, turned, diag):
    leaves, slots = near_cols.shape
    size = near_blocks.shape[2]
    block = diag.shape[1]
    whole = pl.BlockSpec(memory_space=pltpu.VMEM)
    scalar = pl.BlockSpec(memory_space=pltpu.SMEM)
    return pl.pallas_call(
        near_kernel,
        in_specs=[scalar, scalar, scalar, pl.BlockSpec(memory_space=pl.ANY), whole, whole, whole, whole],
        out_specs=whole,
        out_shape=jax.ShapeDtypeStruct((leaves, slots, block, block), F32),
        scratch_shapes=[
            pltpu.VMEM((DEPTH, size, size), BF16),
            pltpu.SemaphoreType.DMA((DEPTH,)),
        ],
        compiler_params=pltpu.CompilerParams(vmem_limit_bytes=40 << 20),
        name="near_stage",
    )(near_cols, near_count, base, near_blocks, own_rows, skel, turned, diag)


def top_kernel(first_ref, second_ref, coupling_ref, basis_ref, factor_ref, schur_ref, merged, rotated):
    block = first_ref.shape[0]
    merged[:block, :block] = first_ref[...]
    merged[:block, block:] = coupling_ref[...]
    merged[block:, :block] = coupling_ref[...].T
    merged[block:, block:] = second_ref[...]
    basis = basis_ref[...]
    high, low = split(merged[...])
    high, low = split(mul(high, basis, NN) + mul(low, basis, NN))
    left = basis.T
    rotated[...] = mul(left, high, NN) + mul(left, low, NN)
    lowers, inverses = factor_blocks([rotated[:block, :block]])
    factor_ref[...] = lowers[0]
    tail = mul_three(rotated[block:, :block], inverses[0], NT)
    schur_ref[...] = rotated[block:, block:] - mul_three(tail, tail, NT)


def top_stage(first_block, second_block, coupling, basis):
    block = coupling.shape[0]
    whole = pl.BlockSpec(memory_space=pltpu.VMEM)
    return pl.pallas_call(
        top_kernel,
        in_specs=[whole] * 4,
        out_specs=[whole] * 2,
        out_shape=[jax.ShapeDtypeStruct((block, block), F32)] * 2,
        scratch_shapes=[
            pltpu.VMEM((2 * block, 2 * block), F32),
            pltpu.VMEM((2 * block, 2 * block), F32),
        ],
        cost_estimate=pl.CostEstimate(
            flops=10_000_000_000, bytes_accessed=600_000, transcendentals=0
        ),
        name="top_stage",
    )(first_block, second_block, coupling, basis)


def local(near_blocks, leaf_basis, near_cols, near_count, children, parent_basis, far_coupling):
    local_leaves = near_cols.shape[0]
    block = far_coupling.shape[1]
    red_size = leaf_basis.shape[1] - block
    row_index = lax.axis_index("row")
    col_index = lax.axis_index("col")
    col_count = lax.axis_size("col")
    row_count = lax.axis_size("row")
    group_size = local_leaves * col_count
    group_base = row_index * group_size
    skel = lax.all_gather(leaf_basis[:, :, red_size:], "col", axis=0, tiled=True)
    factors, diag_schur, rows = leaf_stage(near_blocks, leaf_basis, block)
    child_all = lax.all_gather(diag_schur, "col", axis=0, tiled=True)
    turned = lax.all_gather(rows[:, block:, :], "col", axis=0, tiled=True)
    partner_row = row_index + 1 - 2 * (row_index % 2)
    parent_id = row_index * col_count + col_index
    first_block = child_all[children[parent_id, 0] - group_base]
    partner_parent = partner_row * col_count + col_index
    outgoing = child_all[children[partner_parent, 1] - group_base]
    route = [(r, r ^ 1) for r in range(row_count)]
    second_block = lax.ppermute(outgoing, "row", route)
    top_factor, top_schur = top_stage(first_block, second_block, far_coupling[0], parent_basis[0])
    base = jnp.reshape(group_base, (1,)).astype(jnp.int32)
    near_schur = near_stage(
        near_blocks, near_cols, near_count, base, rows, skel, turned, diag_schur
    )
    return (factors, near_schur, top_factor[None], top_schur[None])


def solution(mesh):
    placed = (
        P(("row", "col"), None, None, None),
        P(("row", "col"), None, None),
        P(("row", "col"), None),
        P(("row", "col")),
        P(),
        P(("row", "col"), None, None),
        P(("row", "col"), None, None),
    )
    return jax.shard_map(
        local,
        mesh=mesh,
        in_specs=placed,
        out_specs=(
            P(("row", "col"), None, None),
            P(("row", "col"), None, None, None),
            P(("row", "col"), None, None),
            P(("row", "col"), None, None),
        ),
        check_vma=False,
    )
```

time: 591 us -> 204 us (0.35)
  other arithmetic: 220 us -> 0 us
  matrix products: 159 us -> 0 us
  local copies, waits for them, and re-layouts: 78.3 us -> 9.53 us
  Pallas kernels: 0 us -> 45.6 us
  waiting for transfers between devices: 89.7 us -> 130 us
  loops' own time: 22.6 us -> 0 us
    another operation x23 -> x0, other arithmetic: 214 us -> none  [the longest x13 124 us: rotate_pivot(): factor = jnp.linalg.cholesky(rotated[:red_size, :red_size])]
    dot_general x157 -> x0, matrix products: 141 us -> none  [the longest x30 42.3 us: pair_folded(): jnp.dot(near_block, other_panel, preferred_element_type=jnp.float32)]
    pallas_call x0 -> x3, Pallas kernels: none -> 45.6 us  [the longest x1 33.7 us: leaf_stage(): pl.pallas_call(leaf_kernel, grid=(1,), in_specs=[pl.BlockSpec((leaves, 1,...]
    all_gather x1, waiting for transfers between devices: 22.3 us -> 49.8 us  [local(): turned = lax.all_gather(rows[:, block:, :], 'col', axis=0, tiled=True)]
    another operation x3 -> x0, loops' own time: 22.6 us -> none  [the longest x2 22.6 us: local(): lax.map(slot_term, (near_blocks[local_leaf, 1:], near_cols[local_leaf, 1:]))]
    dynamic_slice x31 -> x1, local copies, waits for them, and re-layouts: 20.5 us -> 0.59 us  [local(): outgoing = child_all[children[partner_parent, 1] - group_base]]
    another operation x16 -> x0, matrix products: 17.6 us -> none  [the longest x10 9.67 us: rotate_pivot(): jax.scipy.linalg.cho_solve((factor, True), rotated[:red_size, red_size:])]
    all_gather x1, waiting for transfers between devices: 21.5 us -> 38.5 us  [local(): child_all = lax.all_gather(diag_schur, 'col', axis=0, tiled=True)]
  transfers between devices with their start and end apart: 4 -> 4, of which waited for: 4 -> 4; matrix products, arithmetic and copies ran while one was open for 9% -> 2% of each run, Pallas kernels for 0% -> 3%
where the time goes in v1:
time: 204 us; the launch traced here: 201 us
  waiting for transfers between devices  130 us (64%)
  Pallas kernels  45.6 us (22%)
  between operations  15.1 us (7%)
  local copies, waits for them, and re-layouts  9.53 us (5%)
    all_gather x1, waiting for transfers between devices, local(): turned = lax.all_gather(rows[:, block:, :], 'col', axis=0, tiled=True)  49.8 us
    all_gather x1, waiting for transfers between devices, local(): lax.all_gather(leaf_basis[:, :, red_size:], 'col', axis=0, tiled=True)  40.5 us
    all_gather x1, waiting for transfers between devices, local(): child_all = lax.all_gather(diag_schur, 'col', axis=0, tiled=True)  38.5 us
    pallas_call x1, Pallas kernels, leaf_stage(): pl.pallas_call(leaf_kernel, grid=(1,), in_specs=[pl.BlockSpec((leaves, 1,...  33.7 us
    pallas_call x1, Pallas kernels, top_stage(): pl.pallas_call(top_kernel, in_specs=[whole] * 4, out_specs=[whole] * 2, o...  6.67 us
    pallas_call x1, Pallas kernels, near_stage(): pl.pallas_call(near_kernel, in_specs=[scalar, scalar, scalar, pl.BlockSpe...  5.21 us
    unnamed x14, local copies, waits for them, and re-layouts  5.04 us
  transfers between devices with their start and end apart: 4, of which 4 were waited for; matrix products, arithmetic and copies ran while one was open for 2% of the time, Pallas kernels for 3%

profile of v1, /device:TPU:0, one launch (start us, length us, event | category | flops | bytes accessed | tf_op | source)
XLA Modules:
  0.0 200.7 jit_solution(2838922465901873022)
XLA Ops:
  7.2 0.0 all-gather.8.cloned.1.call-start
  7.2 0.0 copy-start.2
  7.2 1.2 copy-done.2
  8.4 0.0 copy-start.5
  8.4 33.7 %leaf_stage.1 = (f32[2,384,384]{2,1,0:T(8,128)}, f32[2,128,128]{2,1,0:T(8,128)}, bf16[2,256,512]{2,1,0:T(8,128)(2,1)S(1)}) custom-call(bf16[2,16,512,512]{3,2,1,0:T(8,128)(2,1)} %near_ref.3, bf16[2,512,512]{2,1,0:T(8,128)(2,1)S(1)} %copy-done.2), custom_call_target="tpu_custom_call" | custom-call | flops 40000000000 | bytes 6000000 | tf_op jit(solution)/shard_map/leaf_stage/pallas_call | solution.py:165
  42.2 0.0 all-gather.8.cloned.1.call-update
  42.2 0.0 all-gather.4.cloned.1.call-start
  42.2 1.7 slice.6
  43.9 0.0 all-gather.4.cloned.1.call-update
  43.9 0.2 all-gather.6.cloned.1.call-start
  44.2 0.7 slice.7
  44.9 0.0 all-gather.6.cloned.1.call-update
  44.9 0.0 copy-done.5
  45.0 0.6 constant_dynamic-slice_fusion.1
  46.9 38.5 %all-gather.8.cloned.1.call-done = f32[16,128,128]{2,1,0:T(8,128)} async-done(((f32[2,128,128]{2,1,0:T(8,128)}), f32[16,128,128]{2,1,0:T(8,128)}) %all-gather.8.cloned.1.call-update) | async-done | bytes 1048592 | tf_op jit(solution)/shard_map/all_gather | solution.py:320
  85.3 1.5 dynamic-slice_bitcast_fusion
  86.9 0.0 collective-permute-start
  86.9 1.3 collective-permute-done.second_ref
  88.1 0.0 copy-start.6
  88.1 0.6 copy-done.6
  88.7 0.0 copy-start.3
  88.7 0.0 copy-start.4
  88.7 6.7 %top_stage.1 = (f32[128,128]{1,0:T(8,128)}, f32[128,128]{1,0:T(8,128)}) custom-call(f32[128,128]{1,0:T(8,128)} %get-tuple-element.15.first_ref, f32[128,128]{1,0:T(8,128)} %copy-done.6, f32[128,128]{1,0:T(8,128)} %bitcast.12, bf16[256,256]{1,0:T(8,128)(2,1)} %bitcast.11), custom_call_target="tpu_custom_call" | custom-call | flops 10000000000 | bytes 600000 | tf_op jit(solution)/shard_map/top_stage/pallas_call | solution.py:292
  95.4 40.5 %all-gather.4.cloned.1.call-done.skel_ref = bf16[16,512,128]{2,1,0:T(8,128)(2,1)} async-done(((bf16[2,512,128]{2,1,0:T(8,128)(2,1)}), bf16[16,512,128]{2,1,0:T(8,128)(2,1)}) %all-gather.4.cloned.1.call-update) | async-done | bytes 2097168 | tf_op jit(solution)/shard_map/all_gather | solution.py:318
  135.9 49.8 %all-gather.6.cloned.1.call-done.turned_ref = bf16[16,128,512]{2,1,0:T(8,128)(2,1)} async-done(((bf16[2,128,512]{2,1,0:T(8,128)(2,1)}), bf16[16,128,512]{2,1,0:T(8,128)(2,1)}) %all-gather.6.cloned.1.call-update) | async-done | bytes 2097168 | tf_op jit(solution)/shard_map/all_gather | solution.py:321
  185.7 0.0 copy-done.3
  185.7 0.0 copy-done.4
  185.7 0.0 copy-start
  185.7 1.6 copy-done
  187.3 0.0 copy-start.1
  187.3 1.6 copy-done.1
  188.9 5.2 %near_stage.1 = f32[2,16,128,128]{3,2,1,0:T(8,128)} custom-call(s32[2,16]{1,0:T(2,128)S(1)} %copy-done.3, s32[2]{0:T(128)S(1)} %copy-done.4, s32[1]{0:T(128)} %bitcast.base_ref, bf16[2,16,512,512]{3,2,1,0:T(8,128)(2,1)} %near_ref.3, bf16[2,256,512]{2,1,0:T(8,128)(2,1)S(1)} %get-tuple-element.10.own_ref, bf16[16,512,128]{2,1,0:T(8,128)(2,1)S(1)} %copy-done, ...), custom_call_target="tpu_custom_call" | custom-call | tf_op jit(solution)/shard_map/near_stage/pallas_call | solution.py:258
Async XLA Ops:
  7.2 78.2 %all-gather.8.cloned.1.call-start = ((), (), s32[]{:S(2)}) async-start(), calls=%async_computation.2 | async-start | bytes 1179648 | tf_op jit(solution)/shard_map/all_gather | solution.py:320
  7.2 1.2 copy-start.2
  8.4 36.5 %copy-start.5 = (s32[32,2]{0,1:T(2,128)S(1)}, s32[32,2]{0,1:T(2,128)}, u32[]{:S(2)}) copy-start(s32[32,2]{0,1:T(2,128)} %param.11) | copy-start | bytes 772
  42.2 93.7 %all-gather.4.cloned.1.call-start = ((), (), s32[]{:S(2)}) async-start(), calls=%async_computation | async-start | bytes 2359296 | tf_op jit(solution)/shard_map/all_gather | solution.py:318
  43.9 141.8 %all-gather.6.cloned.1.call-start = ((), (), s32[]{:S(2)}) async-start(), calls=%async_computation.1 | async-start | bytes 2359296 | tf_op jit(solution)/shard_map/all_gather | solution.py:321
  86.9 1.3 collective-permute-start
  88.1 0.6 copy-start.6
  88.7 97.0 %copy-start.3 = (s32[2,16]{1,0:T(2,128)S(1)}, s32[2,16]{1,0:T(2,128)}, u32[]{:S(2)}) copy-start(s32[2,16]{1,0:T(2,128)} %cols_ref.1) | copy-start | bytes 388
  88.7 97.0 %copy-start.4 = (s32[2]{0:T(128)S(1)}, s32[2]{0:T(128)}, u32[]{:S(2)}) copy-start(s32[2]{0:T(128)} %count_ref.1) | copy-start | bytes 28
  185.7 1.6 copy-start
  187.3 1.6 copy-start.1
Sparse Core Ops, SparseCore 0:
  42.3 42.9 all-gather.7
  88.0 47.8 all-gather.3
  138.1 47.6 all-gather.5
